TPU v7x, 32 devices: a whole 2x2x4 slice. The times are simulated.
32 devices in a mesh: groups: 2 (over y), seq: 4 (over z), mp: 4 (over x, core).
Axes of the slice: x: 2, y: 2, z: 4, core: 2. Of those that a mesh axis runs over, the one named last changes fastest.
Arguments:
- node_vectors: bfloat16 [1024, 2048], P(('groups', 'seq'), 'mp'), parts along dimension 0, may hold values from -6 to 6
- standardize_multiplier: float32 [2048], replicated, may hold values from 0.1 to 1.9
- probe_matrix: bfloat16 [2048, 1024], P(None, 'mp'), may hold values from -1 to 1
- lookup_matrix: bfloat16 [2048, 1024], P(None, 'mp'), may hold values from -1 to 1
- content_matrix: bfloat16 [2048, 1024], P(None, 'mp'), may hold values from -0.125 to 0.125
- softness_per_group: float32 [8], P('mp'), may hold values from 0.5 to 12
- exit_matrix: bfloat16 [1024, 2048], P('mp'), may hold values from -0.1875 to 0.1875
Outputs:
- mixed: bfloat16 [1024, 2048], P(('groups', 'seq'), 'mp'), parts along dimension 0
There are 2 independent parts, one for each index of `groups`. A program takes and returns all parts, laid end to end along the dimension named above; an argument that names none is the same for every part. Nothing has to cross between parts.
All inputs are finite; a program needn't handle non-finite values.
Results may differ from a plain program's by a relative error of at most 0.011.
Values may be sent and summed in bfloat16 or wider, within the bound.
A program may use at most 64 MiB of HBM per device.

v0:
```python
import math

import jax
import jax.numpy as jnp
from jax import lax
from jax.sharding import PartitionSpec as P


def attend(state_in, blocks, query_heads, inverse_root_span, resident_groups, channel_span):
    running_max, running_sum, weighted = state_in
    key_block, value_block = blocks
    count = key_block.shape[0]
    key_heads = key_block.reshape(count, resident_groups, channel_span)
    value_heads = value_block.reshape(count, resident_groups, channel_span)
    scores = (
        jnp.einsum("rhd,nhd->hrn", query_heads, key_heads, preferred_element_type=jnp.float32)
        * inverse_root_span[:, None, None]
    )
    new_max = jnp.max(scores, axis=-1)
    rescale = jnp.exp(running_max - new_max)
    weights = jnp.exp(scores - new_max[:, :, None])
    running_sum = running_sum * rescale + jnp.sum(weights, axis=-1)
    update = jnp.einsum(
        "hrn,nhd->hrd",
        weights.astype(jnp.bfloat16),
        value_heads,
        preferred_element_type=jnp.float32,
    )
    weighted = weighted * rescale[:, :, None] + update
    return (new_max, running_sum, weighted)


def per_device(
    node_vectors,
    standardize_multiplier,
    probe_matrix,
    lookup_matrix,
    content_matrix,
    softness_per_group,
    exit_matrix,
):
    full_rows = lax.all_gather(node_vectors, "mp", axis=1, tiled=True)
    widened = full_rows.astype(jnp.float32)
    average = jnp.mean(widened, axis=-1, keepdims=True)
    centered = widened - average
    variance = jnp.mean(centered * centered, axis=-1, keepdims=True)
    normed = (centered * lax.rsqrt(variance + 1e-05) * standardize_multiplier).astype(jnp.bfloat16)
    queries = jnp.dot(normed, probe_matrix, preferred_element_type=jnp.float32).astype(jnp.bfloat16)
    key_rows = jnp.dot(normed, lookup_matrix, preferred_element_type=jnp.float32).astype(
        jnp.bfloat16
    )
    value_rows = jnp.dot(normed, content_matrix, preferred_element_type=jnp.float32).astype(
        jnp.bfloat16
    )
    resident_groups = softness_per_group.shape[0]
    head_cols = queries.shape[1]
    channel_span = head_cols // resident_groups
    token_count = queries.shape[0]
    query_heads = queries.reshape(token_count, resident_groups, channel_span)
    inverse_root_span = softness_per_group / math.sqrt(channel_span)
    initial = (
        jnp.full((resident_groups, token_count), -jnp.inf, jnp.float32),
        jnp.zeros((resident_groups, token_count), jnp.float32),
        jnp.zeros((resident_groups, token_count, channel_span), jnp.float32),
    )
    final = attend(
        initial,
        (
            lax.all_gather(key_rows, "seq", axis=0, tiled=True),
            lax.all_gather(value_rows, "seq", axis=0, tiled=True),
        ),
        query_heads,
        inverse_root_span,
        resident_groups,
        channel_span,
    )
    heads_out = (
        (final[2] / final[1][:, :, None])
        .transpose(1, 0, 2)
        .reshape(token_count, head_cols)
        .astype(jnp.bfloat16)
    )
    partial_sums = jnp.dot(heads_out, exit_matrix, preferred_element_type=jnp.float32)
    summed = lax.psum_scatter(
        partial_sums.astype(jnp.bfloat16), "mp", scatter_dimension=1, tiled=True
    ).astype(jnp.float32)
    return (node_vectors.astype(jnp.float32) + summed).astype(jnp.bfloat16)


def solution(mesh):
    return jax.shard_map(
        per_device,
        mesh=mesh,
        in_specs=(
            P(("groups", "seq"), "mp"),
            P(),
            P(None, "mp"),
            P(None, "mp"),
            P(None, "mp"),
            P("mp"),
            P("mp", None),
        ),
        out_specs=P(("groups", "seq"), "mp"),
        check_vma=False,
    )
```

profile of v0, /device:TPU:0, one launch (start us, length us, event | category | flops | bytes accessed | tf_op | source)
XLA Modules:
  0.0 81.6 jit_solution(14585379958456140718)
XLA Ops:
  6.5 0.0 copy-start
  6.5 0.0 copy-start.2
  6.5 0.0 reduce-scatter.2.cloned.1.call-start
  6.5 0.8 broadcast_multiply_fusion
  7.3 8.8 %all_gather.9 = bf16[128,2048]{1,0:T(8,128)(2,1)S(1)} all-gather(bf16[128,512]{1,0:T(8,128)(2,1)} %param.7), channel_id=1, replica_groups=mesh['groups'=2,'seq'=4,'mp'=4] {'mp'}, dimensions={1}, use_global_device_ids=true | all-gather | bytes 655360 | tf_op jit(solution)/shard_map/all_gather | solution.py:42
  16.2 0.2 convert_reduce_fusion
  16.4 0.0 copy-start.5
  16.4 0.3 fusion.6
  16.7 0.0 copy-done.2
  16.7 0.4 copy-done.5
  17.1 0.0 copy-start.3
  17.1 0.4 convolution_convert_fusion.2
  17.4 0.9 %copy-done.3 = bf16[2048,256]{1,0:T(8,128)(2,1)S(1)} copy-done((bf16[2048,256]{1,0:T(8,128)(2,1)S(1)}, bf16[2048,256]{1,0:T(8,128)(2,1)}, u32[]{:S(2)}) %copy-start.3) | copy-done | bytes 1048600
  18.3 0.0 copy-start.4
  18.3 0.4 convolution_convert_fusion.1
  18.6 0.9 %copy-done.4 = bf16[2048,256]{1,0:T(8,128)(2,1)S(1)} copy-done((bf16[2048,256]{1,0:T(8,128)(2,1)S(1)}, bf16[2048,256]{1,0:T(8,128)(2,1)}, u32[]{:S(2)}) %copy-start.4) | copy-done | bytes 1048600
  19.5 0.4 fusion.5
  19.9 14.1 %all_gather.11 = bf16[512,256]{1,0:T(8,128)(2,1)S(1)} all-gather(bf16[128,256]{1,0:T(8,128)(2,1)S(1)} %convolution_convert_fusion.1), channel_id=1, replica_groups=mesh['groups'=2,'seq'=4,'mp'=4] {'seq'}, dimensions={0}, use_global_device_ids=true | all-gather | bytes 327680 | tf_op jit(solution)/shard_map/all_gather | solution.py:70
  34.0 0.1 copy.11
  34.1 14.6 %all_gather.10 = bf16[512,256]{1,0:T(8,128)(2,1)S(1)} all-gather(bf16[128,256]{1,0:T(8,128)(2,1)S(1)} %convolution_convert_fusion.2), channel_id=1, replica_groups=mesh['groups'=2,'seq'=4,'mp'=4] {'seq'}, dimensions={0}, use_global_device_ids=true | all-gather | bytes 327680 | tf_op jit(solution)/shard_map/all_gather | solution.py:69
  48.7 0.3 fusion.20
  49.1 0.2 fusion.9
  49.3 0.3 fusion.4
  49.6 0.0 copy-done
  49.6 1.1 %convolution_convert_fusion = bf16[128,2048]{1,0:T(8,128)(2,1)} fusion(bf16[128,256]{0,1:T(8,128)(2,1)S(1)} %bitcast.39, bf16[256,2048]{1,0:T(8,128)(2,1)S(1)} %copy-done), kind=kOutput, calls=%fused_computation | convolution fusion | flops 134479872 | bytes 1638400 | tf_op jit(solution)/shard_map/dot_general | solution.py:83
  50.8 0.0 copy-start.1
  50.8 0.0 reduce-scatter.2.cloned.1.call-update
  50.8 22.4 %reduce-scatter.2.cloned.1.call-done = bf16[128,512]{1,0:T(8,128)(2,1)} async-done(((bf16[128,2048]{1,0:T(8,128)(2,1)}), bf16[128,512]{1,0:T(8,128)(2,1)}) %reduce-scatter.2.cloned.1.call-update) | async-done | bytes 131088 | tf_op jit(solution)/shard_map/reduce_scatter | solution.py:84
  73.2 0.0 copy-done.1
  73.2 1.6 %add_convert_fusion = bf16[128,512]{1,0:T(8,128)(2,1)} fusion(bf16[128,512]{1,0:T(8,128)(2,1)} %reduce-scatter.2.cloned.1.call-done, bf16[128,512]{1,0:T(8,128)(2,1)S(1)} %copy-done.1), kind=kLoop, calls=%fused_computation.22 | loop fusion | flops 262144 | bytes 393216 | tf_op jit(solution)/shard_map/convert_element_type | solution.py:87
  (4 shorter events, 0.0 us)
Async XLA Ops:
  6.5 43.1 %copy-start = (bf16[256,2048]{1,0:T(8,128)(2,1)S(1)}, bf16[256,2048]{1,0:T(8,128)(2,1)}, u32[]{:S(2)}) copy-start(bf16[256,2048]{1,0:T(8,128)(2,1)} %param.13) | copy-start | bytes 3145732
  6.5 10.1 %copy-start.2 = (bf16[2048,256]{1,0:T(8,128)(2,1)S(1)}, bf16[2048,256]{1,0:T(8,128)(2,1)}, u32[]{:S(2)}) copy-start(bf16[2048,256]{1,0:T(8,128)(2,1)} %param.10) | copy-start | bytes 3145732
  6.5 66.6 %reduce-scatter.2.cloned.1.call-start = ((), (), s32[]{:S(2)}) async-start(), calls=%async_computation.1 | async-start | bytes 655360 | tf_op jit(solution)/shard_map/reduce_scatter | solution.py:84
  16.4 0.7 copy-start.5
  17.1 1.2 %copy-start.3 = (bf16[2048,256]{1,0:T(8,128)(2,1)S(1)}, bf16[2048,256]{1,0:T(8,128)(2,1)}, u32[]{:S(2)}) copy-start(bf16[2048,256]{1,0:T(8,128)(2,1)} %param.11) | copy-start | bytes 3145732
  18.3 1.2 %copy-start.4 = (bf16[2048,256]{1,0:T(8,128)(2,1)S(1)}, bf16[2048,256]{1,0:T(8,128)(2,1)}, u32[]{:S(2)}) copy-start(bf16[2048,256]{1,0:T(8,128)(2,1)} %param.9) | copy-start | bytes 3145732
  50.8 22.4 %copy-start.1 = (bf16[128,512]{1,0:T(8,128)(2,1)S(1)}, bf16[128,512]{1,0:T(8,128)(2,1)}, u32[]{:S(2)}) copy-start(bf16[128,512]{1,0:T(8,128)(2,1)} %param.7) | copy-start | bytes 393220
Sparse Core Ops, SparseCore 0:
  50.9 22.2 reduce-scatter.1
where the time goes:
time: 81.9 us; the launch traced here: 81.6 us
  blocking collectives  37.6 us (46%)
  waiting for transfers between devices  22.4 us (27%)
  between operations  13.5 us (16%)
  other arithmetic  3.1 us (4%)
  matrix products  2.85 us (3%)
  local copies, waits for them, and re-layouts  2.25 us (3%)
    reduce_scatter x1, waiting for transfers between devices, per_device(): lax.psum_scatter(partial_sums.astype(jnp.bfloat16), 'mp', scatter_dimensi...  22.4 us
    all_gather x1, blocking collectives, per_device(): lax.all_gather(key_rows, 'seq', axis=0, tiled=True)  14.6 us
    all_gather x1, blocking collectives, per_device(): lax.all_gather(value_rows, 'seq', axis=0, tiled=True)  14.1 us
    all_gather x1, blocking collectives, per_device(): full_rows = lax.all_gather(node_vectors, 'mp', axis=1, tiled=True)  8.84 us
    unnamed x12, local copies, waits for them, and re-layouts  2.11 us
  transfers between devices with their start and end apart: 1, of which 1 were waited for; matrix products, arithmetic and copies ran while one was open for 0% of the time, Pallas kernels for 0%

commit v1 on v0

v1 whole, which is shorter than its diff:
```python
import functools
import math

import jax
import jax.numpy as jnp
from jax import lax
from jax.experimental import pallas as pl
from jax.experimental.pallas import tpu as pltpu
from jax.sharding import PartitionSpec as P

MESH = pl.DeviceIdType.MESH
F32 = jnp.float32
BF16 = jnp.bfloat16
UNROLL_LIMIT = 8


def remote(src, dst, send_sem, recv_sem, axis, index):
    return pltpu.make_async_remote_copy(
        src_ref=src,
        dst_ref=dst,
        send_sem=send_sem,
        recv_sem=recv_sem,
        device_id={axis: index},
        device_id_type=MESH,
    )


def each(count, body):
    if count <= UNROLL_LIMIT:
        for i in range(count):
            body(i)
    else:
        lax.fori_loop(0, count, lambda i, c: (body(i), c)[1], 0)


def kernel(
    n_mp,
    n_seq,
    softness_ref,
    x_hbm,
    gain_ref,
    wq_hbm,
    wk_hbm,
    wv_hbm,
    wo_hbm,
    out_ref,
    xg,
    wq,
    wk,
    wv,
    wo,
    normed,
    q_ref,
    kv,
    scores,
    heads,
    out_send,
    out_recv,
    w_sem,
    x_sem,
    xg_send,
    xg_recv,
    kv_send,
    kv_recv,
    rs_send,
    rs_recv,
):
    me = lax.axis_index("mp")
    spot = lax.axis_index("seq")
    rows, part = x_hbm.shape
    head_cols = wq_hbm.shape[1]
    groups = softness_ref.shape[0]
    span = head_cols // groups
    paired = n_mp == 4
    has_left = spot > 0
    has_right = spot < n_seq - 1

    own_x = pltpu.make_async_copy(x_hbm, xg.at[me], x_sem)
    own_x.start()
    loads = [
        pltpu.make_async_copy(src, dst, w_sem.at[i])
        for i, (src, dst) in enumerate(((wk_hbm, wk), (wv_hbm, wv), (wq_hbm, wq), (wo_hbm, wo)))
    ]
    for load in loads:
        load.start()

    barrier = pltpu.get_barrier_semaphore()
    for step in range(1, n_mp):
        pl.semaphore_signal(
            barrier, inc=1, device_id={"mp": lax.rem(me + step, n_mp)}, device_id_type=MESH
        )

    @pl.when(has_left)
    def _():
        pl.semaphore_signal(barrier, inc=1, device_id={"seq": spot - 1}, device_id_type=MESH)

    @pl.when(has_right)
    def _():
        pl.semaphore_signal(barrier, inc=1, device_id={"seq": spot + 1}, device_id_type=MESH)

    pl.semaphore_wait(
        barrier, n_mp - 1 + has_left.astype(jnp.int32) + has_right.astype(jnp.int32)
    )

    if paired:
        near = me + 1 - 2 * lax.rem(me, 2)
        far = lax.rem(me + 2, 4)
        cross = lax.rem(near + 2, 4)
        half = rows // 2
        pieces = [pl.ds(0, half), pl.ds(half, half)]
        sends = []
        for c, piece in enumerate(pieces):
            sends.append(
                remote(x_hbm.at[piece], xg.at[me, piece], xg_send.at[0, c], xg_recv.at[0, c], "mp", far)
            )
        for c, piece in enumerate(pieces):
            sends.append(
                remote(x_hbm.at[piece], xg.at[me, piece], xg_send.at[1, c], xg_recv.at[1, c], "mp", near)
            )
        for send in sends:
            send.start()
        for c, piece in enumerate(pieces):
            remote(
                xg.at[far, piece], xg.at[far, piece], xg_send.at[0, c], xg_recv.at[0, c], "mp", far
            ).wait_recv()
            relay = remote(
                xg.at[far, piece], xg.at[far, piece], xg_send.at[2, c], xg_recv.at[2, c], "mp", near
            )
            relay.start()
            sends.append(relay)
        for c, piece in enumerate(pieces):
            remote(
                xg.at[near, piece], xg.at[near, piece], xg_send.at[1, c], xg_recv.at[1, c], "mp", near
            ).wait_recv()
        for c, piece in enumerate(pieces):
            remote(
                xg.at[cross, piece], xg.at[cross, piece], xg_send.at[2, c], xg_recv.at[2, c], "mp", near
            ).wait_recv()
    else:
        sends = []
        for step in range(1, n_mp):
            peer = lax.rem(me + step, n_mp)
            send = remote(
                x_hbm, xg.at[me], xg_send.at[step, 0], xg_recv.at[step, 0], "mp", peer
            )
            send.start()
            sends.append(send)
        for step in range(1, n_mp):
            source = lax.rem(me - step + n_mp, n_mp)
            remote(
                xg.at[source], xg.at[source], xg_send.at[step, 0], xg_recv.at[step, 0], "mp", source
            ).wait_recv()
    own_x.wait()

    features = n_mp * part
    total = jnp.zeros((rows, 1), F32)
    for j in range(n_mp):
        total = total + jnp.sum(xg[j].astype(F32), axis=-1, keepdims=True)
    average = total / features
    square = jnp.zeros((rows, 1), F32)
    for j in range(n_mp):
        off = xg[j].astype(F32) - average
        square = square + jnp.sum(off * off, axis=-1, keepdims=True)
    inverse = lax.rsqrt(square / features + 1e-05)
    for j in range(n_mp):
        cols = pl.ds(j * part, part)
        off = xg[j].astype(F32) - average
        normed[:, cols] = (off * inverse * gain_ref[:, cols]).astype(BF16)

    for which, (load, weight) in enumerate(((loads[0], wk), (loads[1], wv))):
        load.wait()
        kv[which, spot] = jnp.dot(
            normed[...], weight[...], preferred_element_type=F32
        ).astype(BF16)

        @pl.when(has_right)
        def _():
            remote(
                kv.at[which, spot], kv.at[which, spot],
                kv_send.at[1, which, spot], kv_recv.at[which, spot], "seq", spot + 1,
            ).start()

        @pl.when(has_left)
        def _():
            remote(
                kv.at[which, spot], kv.at[which, spot],
                kv_send.at[0, which, spot], kv_recv.at[which, spot], "seq", spot - 1,
            ).start()

    loads[2].wait()
    q_ref[...] = jnp.dot(normed[...], wq[...], preferred_element_type=F32).astype(BF16)

    def arrive(which, step):
        before = spot - step
        after = spot + step

        @pl.when(before >= 0)
        def _():
            remote(
                kv.at[which, before], kv.at[which, before],
                kv_send.at[1, which, before], kv_recv.at[which, before], "seq", spot - 1,
            ).wait_recv()

            @pl.when(has_right)
            def _():
                remote(
                    kv.at[which, before], kv.at[which, before],
                    kv_send.at[1, which, before], kv_recv.at[which, before], "seq", spot + 1,
                ).start()

        @pl.when(after < n_seq)
        def _():
            remote(
                kv.at[which, after], kv.at[which, after],
                kv_send.at[0, which, after], kv_recv.at[which, after], "seq", spot + 1,
            ).wait_recv()

            @pl.when(has_left)
            def _():
                remote(
                    kv.at[which, after], kv.at[which, after],
                    kv_send.at[0, which, after], kv_recv.at[which, after], "seq", spot - 1,
                ).start()

    def both(i):
        arrive(0, i + 1)
        arrive(1, i + 1)

    if n_seq > 2:
        each(n_seq - 2, both)
    if n_seq > 1:
        arrive(0, n_seq - 1)

    if n_seq <= UNROLL_LIMIT:
        sums, chances = [], []
        for h in range(groups):
            cols = pl.ds(h * span, span)
            keys = kv[0, :, :, cols].reshape(n_seq * rows, span)
            s = lax.dot_general(
                q_ref[:, cols], keys, (((1,), (1,)), ((), ())), preferred_element_type=F32
            ) * (softness_ref[h] / math.sqrt(span))
            top = jnp.max(s, axis=-1, keepdims=True)
            w = jnp.exp(s - top)
            sums.append(jnp.sum(w, axis=-1, keepdims=True))
            chances.append(w.astype(BF16))
        if n_seq > 1:
            arrive(1, n_seq - 1)
        for h in range(groups):
            cols = pl.ds(h * span, span)
            values = kv[1, :, :, cols].reshape(n_seq * rows, span)
            mixed = jnp.dot(chances[h], values, preferred_element_type=F32)
            heads[:, cols] = (mixed / sums[h]).astype(BF16)
    else:
        arrive(1, n_seq - 1)
        for h in range(groups):
            cols = pl.ds(h * span, span)
            factor = softness_ref[h] / math.sqrt(span)

            def first(b, top):
                s = lax.dot_general(
                    q_ref[:, cols], kv[0, b, :, cols], (((1,), (1,)), ((), ())),
                    preferred_element_type=F32,
                ) * factor
                scores[b] = s
                return jnp.maximum(top, jnp.max(s, axis=-1, keepdims=True))

            top = lax.fori_loop(0, n_seq, first, jnp.full((rows, 1), -jnp.inf, F32))

            def second(b, state):
                summed, mixed = state
                w = jnp.exp(scores[b] - top)
                mixed = mixed + jnp.dot(
                    w.astype(BF16), kv[1, b, :, cols], preferred_element_type=F32
                )
                return summed + jnp.sum(w, axis=-1, keepdims=True), mixed

            summed, mixed = lax.fori_loop(
                0, n_seq, second, (jnp.zeros((rows, 1), F32), jnp.zeros((rows, span), F32))
            )
            heads[:, cols] = (mixed / summed).astype(BF16)

    loads[3].wait()

    def share(owner):
        cols = pl.ds(pl.multiple_of(owner * part, part), part)
        return jnp.dot(heads[...], wo[:, cols], preferred_element_type=F32)

    if paired:
        out_send[0] = share(cross).astype(BF16)
        first = remote(out_send.at[0], out_recv.at[0], rs_send.at[0], rs_recv.at[0], "mp", near)
        first.start()
        for_far = share(far)
        out_send[1] = share(near).astype(BF16)
        second = remote(out_send.at[1], out_recv.at[1], rs_send.at[1], rs_recv.at[1], "mp", near)
        second.start()
        first.wait_recv()
        out_send[2] = (for_far + out_recv[0].astype(F32)).astype(BF16)
        third = remote(out_send.at[2], out_recv.at[2], rs_send.at[2], rs_recv.at[2], "mp", far)
        third.start()
        own = share(me) + xg[me].astype(F32)
        second.wait_recv()
        own = own + out_recv[1].astype(F32)
        third.wait_recv()
        out_ref[...] = (own + out_recv[2].astype(F32)).astype(BF16)
        sends.extend((first, second, third))
    else:
        for step in range(1, n_mp):
            peer = lax.rem(me + step, n_mp)
            out_send[step] = share(peer).astype(BF16)
            send = remote(
                out_send.at[step], out_recv.at[step], rs_send.at[step], rs_recv.at[step], "mp", peer
            )
            send.start()
            sends.append(send)
        own = share(me) + xg[me].astype(F32)
        for step in range(1, n_mp):
            remote(
                out_send.at[step], out_recv.at[step], rs_send.at[step], rs_recv.at[step], "mp", me
            ).wait_recv()
            own = own + out_recv[step].astype(F32)
        out_ref[...] = own.astype(BF16)

    for send in sends:
        send.wait_send()

    def drain(b):
        for which in range(2):

            @pl.when(has_right & (b <= spot))
            def _():
                remote(
                    kv.at[which, b], kv.at[which, b],
                    kv_send.at[1, which, b], kv_recv.at[which, b], "seq", spot + 1,
                ).wait_send()

            @pl.when(has_left & (b >= spot))
            def _():
                remote(
                    kv.at[which, b], kv.at[which, b],
                    kv_send.at[0, which, b], kv_recv.at[which, b], "seq", spot - 1,
                ).wait_send()

    each(n_seq, drain)


def per_device(n_mp, n_seq, x, gain, wq, wk, wv, softness, wo):
    rows, part = x.shape
    features, head_cols = wq.shape
    span_rows = n_seq if n_seq > UNROLL_LIMIT else 1
    any_space = pl.BlockSpec(memory_space=pl.ANY)
    vmem = pl.BlockSpec(memory_space=pltpu.VMEM)
    slots = max(n_mp, 3)
    return pl.pallas_call(
        functools.partial(kernel, n_mp, n_seq),
        out_shape=jax.ShapeDtypeStruct((rows, part), BF16),
        in_specs=[
            pl.BlockSpec(memory_space=pltpu.SMEM),
            any_space, vmem, any_space, any_space, any_space, any_space,
        ],
        out_specs=vmem,
        scratch_shapes=[
            pltpu.VMEM((n_mp, rows, part), BF16),
            pltpu.VMEM((features, head_cols), BF16),
            pltpu.VMEM((features, head_cols), BF16),
            pltpu.VMEM((features, head_cols), BF16),
            pltpu.VMEM((head_cols, features), BF16),
            pltpu.VMEM((rows, features), BF16),
            pltpu.VMEM((rows, head_cols), BF16),
            pltpu.VMEM((2, n_seq, rows, head_cols), BF16),
            pltpu.VMEM((span_rows, rows, rows), F32),
            pltpu.VMEM((rows, head_cols), BF16),
            pltpu.VMEM((slots, rows, part), BF16),
            pltpu.VMEM((slots, rows, part), BF16),
            pltpu.SemaphoreType.DMA((4,)),
            pltpu.SemaphoreType.DMA,
            pltpu.SemaphoreType.DMA((slots, 2)),
            pltpu.SemaphoreType.DMA((slots, 2)),
            pltpu.SemaphoreType.DMA((2, 2, n_seq)),
            pltpu.SemaphoreType.DMA((2, n_seq)),
            pltpu.SemaphoreType.DMA((slots,)),
            pltpu.SemaphoreType.DMA((slots,)),
        ],
        compiler_params=pltpu.CompilerParams(collective_id=0, has_side_effects=True),
    )(softness, x, gain.reshape(1, features), wq, wk, wv, wo)


def solution(mesh):
    return jax.shard_map(
        functools.partial(per_device, mesh.shape["mp"], mesh.shape["seq"]),
        mesh=mesh,
        in_specs=(
            P(("groups", "seq"), "mp"),
            P(),
            P(None, "mp"),
            P(None, "mp"),
            P(None, "mp"),
            P("mp"),
            P("mp", None),
        ),
        out_specs=P(("groups", "seq"), "mp"),
        check_vma=False,
    )
```

time: 81.9 us -> 32.9 us (0.40)
  blocking collectives: 37.6 us -> 0 us
  Pallas kernels: 0 us -> 31.2 us
  waiting for transfers between devices: 22.4 us -> 0 us
  between operations: 13.5 us -> 0.01 us
  other arithmetic: 3.1 us -> 0 us
  matrix products: 2.85 us -> 0 us
    all_gather x3 -> x0, blocking collectives: 37.6 us -> none  [the longest x1 14.6 us: per_device(): lax.all_gather(key_rows, 'seq', axis=0, tiled=True)]
    pallas_call x0 -> x1, Pallas kernels: none -> 31.2 us  [per_device(): pl.pallas_call(functools.partial(kernel, n_mp, n_seq), out_shape=jax.Shap...]
    reduce_scatter x1 -> x0, waiting for transfers between devices: 22.4 us -> none  [per_device(): lax.psum_scatter(partial_sums.astype(jnp.bfloat16), 'mp', scatter_dimensi...]
    dot_general x6 -> x0, matrix products: 2.85 us -> none  [the longest x1 1.13 us: per_device(): jnp.dot(heads_out, exit_matrix, preferred_element_type=jnp.float32)]
    convert_element_type x1 -> x0, other arithmetic: 1.59 us -> none  [per_device(): return (node_vectors.astype(jnp.float32) + summed).astype(jnp.bfloat16)]
    unnamed x12 -> x1, local copies, waits for them, and re-layouts: 2.11 us -> 1.57 us
  transfers between devices with their start and end apart: 1 -> 0, of which waited for: 1 -> 0; matrix products, arithmetic and copies ran while one was open for 0% -> 0% of each run, Pallas kernels for 0% -> 0%
where the time goes in v1:
time: 32.9 us; the launch traced here: 32.7 us
  Pallas kernels  31.2 us (95%)
  local copies, waits for them, and re-layouts  1.57 us (5%)
    pallas_call x1, Pallas kernels, per_device(): pl.pallas_call(functools.partial(kernel, n_mp, n_seq), out_shape=jax.Shap...  31.2 us
    unnamed x1, local copies, waits for them, and re-layouts  1.57 us

profile of v1, /device:TPU:0, one launch (start us, length us, event | category | flops | bytes accessed | tf_op | source)
XLA Modules:
  0.0 32.7 jit_solution(1983183632661887343)
XLA Ops:
  0.0 31.2 %shard_map.73 = bf16[128,512]{1,0:T(8,128)(2,1)} custom-call(f32[2]{0:T(128)} %softness_ref.1, bf16[128,512]{1,0:T(8,128)(2,1)} %x_hbm.1, f32[1,2048]{1,0:T(1,128)} %bitcast.1, bf16[2048,256]{1,0:T(8,128)(2,1)} %wq_hbm.1, bf16[2048,256]{1,0:T(8,128)(2,1)} %wk_hbm.1, bf16[2048,256]{1,0:T(8,128)(2,1)} %wv_hbm.1, bf16[256,2048]{1,0:T(8,128)(2,1)} %wo_hbm.1), custom_call_target="tpu_custom_call" | custom-call | tf_op jit(solution)/shard_map/pallas_call | solution.py:353
  31.2 1.6 %copy.9 = bf16[128,512]{1,0:T(8,128)(2,1)} copy(bf16[128,512]{1,0:T(8,128)(2,1)} %shard_map.73) | data formatting | bytes 262144

commit v2 on v1

v2 whole, which is shorter than its diff:
```python
import functools
import math

import jax
import jax.numpy as jnp
from jax import lax
from jax.experimental import pallas as pl
from jax.experimental.pallas import tpu as pltpu
from jax.sharding import PartitionSpec as P

MESH = pl.DeviceIdType.MESH
F32 = jnp.float32
BF16 = jnp.bfloat16
UNROLL_LIMIT = 8
RS_PIECES = 4


def remote(src, dst, send_sem, recv_sem, axis, index):
    return pltpu.make_async_remote_copy(
        src_ref=src,
        dst_ref=dst,
        send_sem=send_sem,
        recv_sem=recv_sem,
        device_id={axis: index},
        device_id_type=MESH,
    )


def each(count, body):
    if count <= UNROLL_LIMIT:
        for i in range(count):
            body(i)
    else:
        lax.fori_loop(0, count, lambda i, c: (body(i), c)[1], 0)


def kernel(
    n_mp,
    n_seq,
    softness_ref,
    x_hbm,
    gain_ref,
    wq_hbm,
    wk_hbm,
    wv_hbm,
    wo_hbm,
    out_ref,
    xg,
    wq,
    wk,
    wv,
    wo,
    normed,
    q_ref,
    kv,
    scores,
    heads,
    out_send,
    out_recv,
    w_sem,
    x_sem,
    xg_send,
    xg_recv,
    kv_send,
    kv_recv,
    rs_send,
    rs_recv,
):
    me = lax.axis_index("mp")
    spot = lax.axis_index("seq")
    rows, part = x_hbm.shape
    head_cols = wq_hbm.shape[1]
    groups = softness_ref.shape[0]
    span = head_cols // groups
    paired = n_mp == 4
    has_left = spot > 0
    has_right = spot < n_seq - 1
    hop = n_seq == 4
    ends = (spot == 0) | (spot == n_seq - 1)

    own_x = pltpu.make_async_copy(x_hbm, xg.at[me], x_sem)
    own_x.start()
    loads = [
        pltpu.make_async_copy(src, dst, w_sem.at[i])
        for i, (src, dst) in enumerate(((wk_hbm, wk), (wv_hbm, wv), (wq_hbm, wq), (wo_hbm, wo)))
    ]
    for load in loads:
        load.start()

    barrier = pltpu.get_barrier_semaphore()
    for step in range(1, n_mp):
        pl.semaphore_signal(
            barrier, inc=1, device_id={"mp": lax.rem(me + step, n_mp)}, device_id_type=MESH
        )

    @pl.when(has_left)
    def _():
        pl.semaphore_signal(barrier, inc=1, device_id={"seq": spot - 1}, device_id_type=MESH)

    @pl.when(has_right)
    def _():
        pl.semaphore_signal(barrier, inc=1, device_id={"seq": spot + 1}, device_id_type=MESH)

    greeted = n_mp - 1 + has_left.astype(jnp.int32) + has_right.astype(jnp.int32)
    if hop:

        @pl.when(ends)
        def _():
            pl.semaphore_signal(
                barrier, inc=1, device_id={"seq": n_seq - 1 - spot}, device_id_type=MESH
            )

        greeted = greeted + ends.astype(jnp.int32)
    pl.semaphore_wait(barrier, greeted)

    half = rows // 2
    pieces = [pl.ds(0, half), pl.ds(half, half)]
    near = me + 1 - 2 * lax.rem(me, 2)
    far = lax.rem(me + 2, n_mp)
    cross = lax.rem(near + 2, n_mp)
    sends = []

    def gather(lane, c, source, target):
        slot = xg.at[source, pieces[c]]
        return remote(slot, slot, xg_send.at[lane, c], xg_recv.at[lane, c], "mp", target)

    if paired:
        for lane, peer in ((0, far), (1, near)):
            for c, piece in enumerate(pieces):
                send = remote(
                    x_hbm.at[piece], xg.at[me, piece],
                    xg_send.at[lane, c], xg_recv.at[lane, c], "mp", peer,
                )
                send.start()
                sends.append(send)
    else:
        for c, piece in enumerate(pieces):
            for step in range(1, n_mp):
                send = remote(
                    x_hbm.at[piece], xg.at[me, piece],
                    xg_send.at[step, c], xg_recv.at[step, c], "mp", lax.rem(me + step, n_mp),
                )
                send.start()
                sends.append(send)
    own_x.wait()

    def relay_far(c):
        if paired:
            gather(0, c, far, far).wait_recv()
            relay = gather(2, c, far, near)
            relay.start()
            sends.append(relay)

    def gathered(c):
        if paired:
            gather(1, c, near, near).wait_recv()
            gather(2, c, cross, near).wait_recv()
        else:
            for step in range(1, n_mp):
                source = lax.rem(me - step + n_mp, n_mp)
                gather(step, c, source, source).wait_recv()

    features = n_mp * part

    def normalize(c):
        piece = pieces[c]
        total = jnp.zeros((half, 1), F32)
        for j in range(n_mp):
            total = total + jnp.sum(xg[j, piece, :].astype(F32), axis=-1, keepdims=True)
        average = total / features
        square = jnp.zeros((half, 1), F32)
        for j in range(n_mp):
            off = xg[j, piece, :].astype(F32) - average
            square = square + jnp.sum(off * off, axis=-1, keepdims=True)
        inverse = lax.rsqrt(square / features + 1e-05)
        for j in range(n_mp):
            cols = pl.ds(j * part, part)
            off = xg[j, piece, :].astype(F32) - average
            normed[piece, cols] = (off * inverse * gain_ref[:, cols]).astype(BF16)

    def block(way, which, owner, c, target):
        slot = kv.at[which, owner, pieces[c]]
        return remote(
            slot, slot, kv_send.at[way, which, owner, c], kv_recv.at[which, owner, c], "seq", target
        )

    def project(which, weight, c):
        kv[which, spot, pieces[c]] = jnp.dot(
            normed[pieces[c], :], weight[...], preferred_element_type=F32
        ).astype(BF16)

        @pl.when(has_right)
        def _():
            block(1, which, spot, c, spot + 1).start()

        @pl.when(has_left)
        def _():
            block(0, which, spot, c, spot - 1).start()

        if hop:

            @pl.when(ends)
            def _():
                block(2, which, spot, c, n_seq - 1 - spot).start()

    relay_far(0)
    gathered(0)
    normalize(0)
    relay_far(1)
    for which, weight in ((0, wk), (1, wv)):
        loads[which].wait()
        project(which, weight, 0)
    gathered(1)
    normalize(1)
    for which, weight in ((0, wk), (1, wv)):
        project(which, weight, 1)
    loads[2].wait()
    q_ref[...] = jnp.dot(normed[...], wq[...], preferred_element_type=F32).astype(BF16)

    def take(which, step, c, forward):
        before = spot - step
        after = spot + step

        @pl.when(before >= 0)
        def _():
            block(1, which, before, c, before).wait_recv()
            if forward:

                @pl.when(has_right)
                def _():
                    block(1, which, before, c, spot + 1).start()

        @pl.when(after < n_seq)
        def _():
            block(0, which, after, c, after).wait_recv()
            if forward:

                @pl.when(has_left)
                def _():
                    block(0, which, after, c, spot - 1).start()

    if hop:
        for c in range(2):
            for which in range(2):
                take(which, 1, c, True)
        for step in (2, 3):
            for c in range(2):
                take(0, step, c, False)

        def last_values():
            for step in (2, 3):
                for c in range(2):
                    take(1, step, c, False)

    else:

        def chain(i):
            for c in range(2):
                for which in range(2):
                    take(which, i + 1, c, True)

        each(n_seq - 1, chain)

        def last_values():
            pass

    if n_seq <= UNROLL_LIMIT:
        sums, chances = [], []
        for h in range(groups):
            cols = pl.ds(h * span, span)
            keys = kv[0, :, :, cols].reshape(n_seq * rows, span)
            s = lax.dot_general(
                q_ref[:, cols], keys, (((1,), (1,)), ((), ())), preferred_element_type=F32
            ) * (softness_ref[h] / math.sqrt(span))
            top = jnp.max(s, axis=-1, keepdims=True)
            w = jnp.exp(s - top)
            sums.append(jnp.sum(w, axis=-1, keepdims=True))
            chances.append(w.astype(BF16))
        last_values()
        for h in range(groups):
            cols = pl.ds(h * span, span)
            values = kv[1, :, :, cols].reshape(n_seq * rows, span)
            mixed = jnp.dot(chances[h], values, preferred_element_type=F32)
            heads[:, cols] = (mixed / sums[h]).astype(BF16)
    else:
        for h in range(groups):
            cols = pl.ds(h * span, span)
            factor = softness_ref[h] / math.sqrt(span)

            def first(b, top):
                s = lax.dot_general(
                    q_ref[:, cols], kv[0, b, :, cols], (((1,), (1,)), ((), ())),
                    preferred_element_type=F32,
                ) * factor
                scores[b] = s
                return jnp.maximum(top, jnp.max(s, axis=-1, keepdims=True))

            top = lax.fori_loop(0, n_seq, first, jnp.full((rows, 1), -jnp.inf, F32))

            def second(b, state):
                summed, mixed = state
                w = jnp.exp(scores[b] - top)
                mixed = mixed + jnp.dot(
                    w.astype(BF16), kv[1, b, :, cols], preferred_element_type=F32
                )
                return summed + jnp.sum(w, axis=-1, keepdims=True), mixed

            summed, mixed = lax.fori_loop(
                0, n_seq, second, (jnp.zeros((rows, 1), F32), jnp.zeros((rows, span), F32))
            )
            heads[:, cols] = (mixed / summed).astype(BF16)

    loads[3].wait()
    rs_pieces = [pl.ds(i * (rows // RS_PIECES), rows // RS_PIECES) for i in range(RS_PIECES)]

    def share(owner):
        cols = pl.ds(pl.multiple_of(owner * part, part), part)
        return jnp.dot(heads[...], wo[:, cols], preferred_element_type=F32)

    if paired:
        quarter = rows // len(rs_pieces)

        def reduce(lane, piece, target):
            return remote(
                out_send.at[lane, piece], out_recv.at[lane, piece],
                rs_send.at[lane, piece.start // quarter], rs_recv.at[lane, piece.start // quarter],
                "mp", target,
            )

        out_send[0] = share(cross).astype(BF16)
        for piece in rs_pieces:
            send = reduce(0, piece, near)
            send.start()
            sends.append(send)
        for_far = share(far)
        for piece in rs_pieces:
            reduce(0, piece, near).wait_recv()
            low = piece.start
            out_send[2, piece] = (
                for_far[low : low + quarter] + out_recv[0, piece].astype(F32)
            ).astype(BF16)
            send = reduce(2, piece, far)
            send.start()
            sends.append(send)
        out_send[1] = share(near).astype(BF16)
        for piece in rs_pieces:
            send = reduce(1, piece, near)
            send.start()
            sends.append(send)
        own = share(me) + xg[me].astype(F32)
        for piece in rs_pieces:
            reduce(1, piece, near).wait_recv()
        own = own + out_recv[1].astype(F32)
        for piece in rs_pieces:
            reduce(2, piece, far).wait_recv()
            low = piece.start
            out_ref[piece, :] = (
                own[low : low + quarter] + out_recv[2, piece].astype(F32)
            ).astype(BF16)
    else:
        for step in range(1, n_mp):
            peer = lax.rem(me + step, n_mp)
            out_send[step] = share(peer).astype(BF16)
            send = remote(
                out_send.at[step], out_recv.at[step], rs_send.at[step, 0], rs_recv.at[step, 0], "mp", peer
            )
            send.start()
            sends.append(send)
        own = share(me) + xg[me].astype(F32)
        for step in range(1, n_mp):
            remote(
                out_send.at[step], out_recv.at[step], rs_send.at[step, 0], rs_recv.at[step, 0], "mp", me
            ).wait_recv()
            own = own + out_recv[step].astype(F32)
        out_ref[...] = own.astype(BF16)

    for send in sends:
        send.wait_send()

    def drain(b):
        for which in range(2):
            for c in range(2):
                to_right = (b == spot) | (b == spot - 1) if hop else b <= spot
                to_left = (b == spot) | (b == spot + 1) if hop else b >= spot

                @pl.when(has_right & to_right)
                def _():
                    block(1, which, b, c, spot + 1).wait_send()

                @pl.when(has_left & to_left)
                def _():
                    block(0, which, b, c, spot - 1).wait_send()

                if hop:

                    @pl.when(ends & (b == spot))
                    def _():
                        block(2, which, b, c, n_seq - 1 - spot).wait_send()

    each(n_seq, drain)


def per_device(n_mp, n_seq, x, gain, wq, wk, wv, softness, wo):
    rows, part = x.shape
    features, head_cols = wq.shape
    span_rows = n_seq if n_seq > UNROLL_LIMIT else 1
    any_space = pl.BlockSpec(memory_space=pl.ANY)
    vmem = pl.BlockSpec(memory_space=pltpu.VMEM)
    slots = max(n_mp, 3)
    return pl.pallas_call(
        functools.partial(kernel, n_mp, n_seq),
        out_shape=jax.ShapeDtypeStruct((rows, part), BF16),
        in_specs=[
            pl.BlockSpec(memory_space=pltpu.SMEM),
            any_space, vmem, any_space, any_space, any_space, any_space,
        ],
        out_specs=vmem,
        scratch_shapes=[
            pltpu.VMEM((n_mp, rows, part), BF16),
            pltpu.VMEM((features, head_cols), BF16),
            pltpu.VMEM((features, head_cols), BF16),
            pltpu.VMEM((features, head_cols), BF16),
            pltpu.VMEM((head_cols, features), BF16),
            pltpu.VMEM((rows, features), BF16),
            pltpu.VMEM((rows, head_cols), BF16),
            pltpu.VMEM((2, n_seq, rows, head_cols), BF16),
            pltpu.VMEM((span_rows, rows, rows), F32),
            pltpu.VMEM((rows, head_cols), BF16),
            pltpu.VMEM((slots, rows, part), BF16),
            pltpu.VMEM((slots, rows, part), BF16),
            pltpu.SemaphoreType.DMA((4,)),
            pltpu.SemaphoreType.DMA,
            pltpu.SemaphoreType.DMA((slots, 2)),
            pltpu.SemaphoreType.DMA((slots, 2)),
            pltpu.SemaphoreType.DMA((3, 2, n_seq, 2)),
            pltpu.SemaphoreType.DMA((2, n_seq, 2)),
            pltpu.SemaphoreType.DMA((slots, RS_PIECES)),
            pltpu.SemaphoreType.DMA((slots, RS_PIECES)),
        ],
        compiler_params=pltpu.CompilerParams(collective_id=0, has_side_effects=True),
    )(softness, x, gain.reshape(1, features), wq, wk, wv, wo)


def solution(mesh):
    return jax.shard_map(
        functools.partial(per_device, mesh.shape["mp"], mesh.shape["seq"]),
        mesh=mesh,
        in_specs=(
            P(("groups", "seq"), "mp"),
            P(),
            P(None, "mp"),
            P(None, "mp"),
            P(None, "mp"),
            P("mp"),
            P("mp", None),
        ),
        out_specs=P(("groups", "seq"), "mp"),
        check_vma=False,
    )
```

time: 32.9 us -> 30.9 us (0.939)
  Pallas kernels: 31.2 us -> 29.1 us
    pallas_call x1, Pallas kernels: 31.2 us -> 29.1 us  [per_device(): pl.pallas_call(functools.partial(kernel, n_mp, n_seq), out_shape=jax.Shap...]
where the time goes in v2:
time: 30.9 us; the launch traced here: 30.7 us
  Pallas kernels  29.1 us (94%)
  local copies, waits for them, and re-layouts  1.57 us (5%)
    pallas_call x1, Pallas kernels, per_device(): pl.pallas_call(functools.partial(kernel, n_mp, n_seq), out_shape=jax.Shap...  29.1 us
    unnamed x1, local copies, waits for them, and re-layouts  1.57 us

profile of v2, /device:TPU:0, one launch (start us, length us, event | category | flops | bytes accessed | tf_op | source)
XLA Modules:
  0.0 30.7 jit_solution(12103201612421405075)
XLA Ops:
  0.0 29.1 %shard_map.73 = bf16[128,512]{1,0:T(8,128)(2,1)} custom-call(f32[2]{0:T(128)} %softness_ref.1, bf16[128,512]{1,0:T(8,128)(2,1)} %x_hbm.1, f32[1,2048]{1,0:T(1,128)} %bitcast.1, bf16[2048,256]{1,0:T(8,128)(2,1)} %wq_hbm.1, bf16[2048,256]{1,0:T(8,128)(2,1)} %wk_hbm.1, bf16[2048,256]{1,0:T(8,128)(2,1)} %wv_hbm.1, bf16[256,2048]{1,0:T(8,128)(2,1)} %wo_hbm.1), custom_call_target="tpu_custom_call" | custom-call | tf_op jit(solution)/shard_map/pallas_call | solution.py:410
  29.1 1.6 %copy.9 = bf16[128,512]{1,0:T(8,128)(2,1)} copy(bf16[128,512]{1,0:T(8,128)(2,1)} %shard_map.73) | data formatting | bytes 262144

commit v3 on v2

--- a/solution.py
+++ b/solution.py
@@ -12,7 +12,7 @@
 F32 = jnp.float32
 BF16 = jnp.bfloat16
 UNROLL_LIMIT = 8
-RS_PIECES = 4
+RS_PIECES = 2
 
 
 def remote(src, dst, send_sem, recv_sem, axis, index):
@@ -188,7 +188,9 @@
         kv[which, spot, pieces[c]] = jnp.dot(
             normed[pieces[c], :], weight[...], preferred_element_type=F32
         ).astype(BF16)
-
+        launch(which, c)
+
+    def launch(which, c):
         @pl.when(has_right)
         def _():
             block(1, which, spot, c, spot + 1).start()
@@ -207,13 +209,15 @@
     gathered(0)
     normalize(0)
     relay_far(1)
-    for which, weight in ((0, wk), (1, wv)):
-        loads[which].wait()
-        project(which, weight, 0)
+    loads[0].wait()
+    project(0, wk, 0)
     gathered(1)
     normalize(1)
-    for which, weight in ((0, wk), (1, wv)):
-        project(which, weight, 1)
+    project(0, wk, 1)
+    loads[1].wait()
+    kv[1, spot] = jnp.dot(normed[...], wv[...], preferred_element_type=F32).astype(BF16)
+    for c in range(2):
+        launch(1, c)
     loads[2].wait()
     q_ref[...] = jnp.dot(normed[...], wq[...], preferred_element_type=F32).astype(BF16)
 
@@ -240,8 +244,8 @@
                     block(0, which, after, c, spot - 1).start()
 
     if hop:
-        for c in range(2):
-            for which in range(2):
+        for which in range(2):
+            for c in range(2):
                 take(which, 1, c, True)
         for step in (2, 3):
             for c in range(2):

time: 30.9 us -> 30.4 us (0.984)
  Pallas kernels: 29.1 us -> 28.7 us
    pallas_call x1, Pallas kernels: 29.1 us -> 28.7 us  [per_device(): pl.pallas_call(functools.partial(kernel, n_mp, n_seq), out_shape=jax.Shap...]
where the time goes in v3:
time: 30.4 us; the launch traced here: 30.2 us
  Pallas kernels  28.7 us (94%)
  local copies, waits for them, and re-layouts  1.57 us (5%)
    pallas_call x1, Pallas kernels, per_device(): pl.pallas_call(functools.partial(kernel, n_mp, n_seq), out_shape=jax.Shap...  28.7 us
    unnamed x1, local copies, waits for them, and re-layouts  1.57 us

profile of v3, /device:TPU:0, one launch (start us, length us, event | category | flops | bytes accessed | tf_op | source)
XLA Modules:
  0.0 30.2 jit_solution(7689287931882800152)
XLA Ops:
  0.0 28.7 %shard_map.73 = bf16[128,512]{1,0:T(8,128)(2,1)} custom-call(f32[2]{0:T(128)} %softness_ref.1, bf16[128,512]{1,0:T(8,128)(2,1)} %x_hbm.1, f32[1,2048]{1,0:T(1,128)} %bitcast.1, bf16[2048,256]{1,0:T(8,128)(2,1)} %wq_hbm.1, bf16[2048,256]{1,0:T(8,128)(2,1)} %wk_hbm.1, bf16[2048,256]{1,0:T(8,128)(2,1)} %wv_hbm.1, bf16[256,2048]{1,0:T(8,128)(2,1)} %wo_hbm.1), custom_call_target="tpu_custom_call" | custom-call | tf_op jit(solution)/shard_map/pallas_call | solution.py:414
  28.7 1.6 %copy.9 = bf16[128,512]{1,0:T(8,128)(2,1)} copy(bf16[128,512]{1,0:T(8,128)(2,1)} %shard_map.73) | data formatting | bytes 262144
